TPU v7x, 256 devices: a whole 4x4x8 slice. The times are simulated.
256 devices in a mesh: pix: 16 (over y_lo, x, core), ion: 16 (over y_hi, z).
Axes of the slice: x: 4, y: 4 (y_hi: 2, y_lo: 2; y = y_hi * 2 + y_lo), z: 8, core: 2. Of those that a mesh axis runs over, the one named last changes fastest.
Arguments:
- images: bfloat16 [20480, 32768], P('ion', 'pix')
- stencil: float32 [5, 32768], P(None, 'pix'), may hold values from 0.05 to 0.4
- pairs: int32 [768, 2], P('ion'), may hold values from 0 to 159, as said below
- live: int32 [16], P('ion'), may hold values from 16 to 48, as said below
- rule_of_block: int32 [160], replicated, may hold values from 0 to 63
- adduct: bfloat16 [64, 128, 128], P('ion'), may hold values from -6 to 6
Outputs:
- smoothed: bfloat16 [20480, 32768], P('ion', 'pix')
- scores: bfloat16 [768, 128, 128], P('ion', 'pix')
Inputs may be any that keep to these rules, and one draw needn't show every extreme that they name: Slot s belongs to ion block range of index s // 48 of ion: a lies in that index's own 20480 // (128 * 16) blocks, and |a - b| <= 3. Entries of unused slots are valid pairs too. `live`: some index of ion uses all its slots.
All inputs are finite; a program needn't handle non-finite values.
Results may differ from a plain program's by a relative error of at most 0.0053.
Values may be sent and summed in bfloat16 or wider, within the bound.
A program may use at most 192 MiB of HBM per device.

v0:
```python
import jax
import jax.numpy as jnp
from jax import lax
from jax.sharding import PartitionSpec as P

REACH = 3
slot_group = 16


def extended_2(array, sides, width):
    for axis, dim in sides:
        size, length = (lax.axis_size(axis), array.shape[dim])
        up = [(i, (i + 1) % size) for i in range(size - 1)]
        down = [(j, i) for i, j in up]
        last = lax.slice_in_dim(array, length - width, length, axis=dim)
        first = lax.slice_in_dim(array, 0, width, axis=dim)
        before = lax.ppermute(last, axis, up)
        after = lax.ppermute(first, axis, down)
        array = jnp.concatenate([before, array, after], axis=dim)
    return array


def on_device(images, stencil, pairs, live, rule_of_block, adduct):
    local_rows, pix_local = images.shape
    block = adduct.shape[1]
    local_blocks = local_rows // block
    padded = extended_2(images, (("pix", 1),), 2)
    total = jnp.zeros((local_rows, pix_local), jnp.float32)
    for tap in range(5):
        total = total + stencil[tap][None, :] * padded[:, tap : tap + pix_local].astype(jnp.float32)
    smoothed = total.astype(jnp.bfloat16)
    extended = extended_2(smoothed, (("ion", 0),), REACH * block)
    values = extended.astype(jnp.float32)
    squares = jnp.sum(values * values, axis=1)
    pixel_count = pix_local * lax.axis_size("pix")
    energy = lax.psum(squares, "pix") / pixel_count
    inverse = 1.0 / jnp.sqrt(energy + 1e-06)
    lookup_tables = lax.all_gather(adduct, "ion", axis=0, tiled=True)
    first = lax.axis_index("ion") * local_blocks
    ext_blocks = extended.reshape(local_blocks + 2 * REACH, block, pix_local)
    inv_blocks = inverse.reshape(local_blocks + 2 * REACH, block)
    slots = pairs.shape[0]
    relative = pairs - first + REACH

    def group_gram(start):
        chosen = lax.dynamic_slice_in_dim(relative, start, slot_group, 0)
        left_operand = jnp.take(ext_blocks, chosen[:, 0], axis=0)
        right_operand = jnp.take(ext_blocks, chosen[:, 1], axis=0)
        return jnp.einsum(
            "uwf,uvf->uwv", left_operand, right_operand, preferred_element_type=jnp.float32
        )

    grams = jnp.concatenate(
        [group_gram(step * slot_group) for step in range(slots // slot_group)], axis=0
    )
    inv_left = jnp.take(inv_blocks, relative[:, 0], axis=0)
    inv_right = jnp.take(inv_blocks, relative[:, 1], axis=0)
    rules = jnp.take(rule_of_block, pairs[:, 1], axis=0)
    matrices = jnp.take(lookup_tables, rules, axis=0)
    share = block // lax.axis_size("pix")
    offset = lax.axis_index("pix") * share
    gram = lax.psum(grams, "pix")
    coloc = (gram * inv_left[:, :, None] * inv_right[:, None, :] / pixel_count).astype(jnp.bfloat16)
    complete_scores = jnp.einsum(
        "src,scd->srd", coloc, matrices, preferred_element_type=jnp.float32
    )
    scores = lax.dynamic_slice_in_dim(complete_scores, offset, share, 1)
    used = jnp.arange(slots, dtype=jnp.int32) < live[0]
    scores = jnp.where(used[:, None, None], scores, 0.0).astype(jnp.bfloat16)
    return (smoothed, scores)


def solution(mesh):
    return jax.shard_map(
        on_device,
        mesh=mesh,
        in_specs=(
            P("ion", "pix"),
            P(None, "pix"),
            P("ion", None),
            P("ion"),
            P(),
            P("ion", None, None),
        ),
        out_specs=(P("ion", "pix"), P("ion", "pix", None)),
        check_vma=False,
    )
```

profile of v0, /device:TPU:7, one launch (start us, length us, event | category | flops | bytes accessed | tf_op | source)
XLA Modules:
  0.0 307.4 jit_solution(16997683368433207593)
XLA Ops:
  8.0 0.0 copy-start
  8.0 0.0 slice-start
  8.0 0.0 copy-start.2
  8.0 0.0 all-gather.2.cloned.1.call-start
  8.1 1.3 fusion.33
  9.4 2.6 collective-permute-start.1
  12.0 0.0 slice-start.1
  12.0 5.4 %collective-permute-start = (bf16[1280,2]{1,0:T(8,128)(2,1)S(1)}, bf16[1280,2]{1,0:T(8,128)(2,1)S(1)}, u32[]{:S(2)}, u32[]{:S(2)}) collective-permute-start(bf16[1280,2]{1,0:T(8,128)(2,1)S(1)} %get-tuple-element.27), channel_id=1, source_target_pairs={{0,16},{16,32},{32,48},{48,64},{64,80},{80,96},{96,112},{112,128},... | collective-permute-start | bytes 15368 | tf_op jit(solution)/shard_map/ppermute | solution.py:17
  17.4 3.0 constant_dynamic-update-slice_fusion.1
  20.4 0.0 copy-done.2
  20.4 0.0 collective-permute-done.1
  20.5 0.1 constant_dynamic-update-slice_fusion
  20.5 0.8 collective-permute-done
  21.4 0.0 slice-done
  21.4 0.0 slice-done.1
  21.4 8.8 %add_convert_fusion = bf16[1280,2048]{1,0:T(8,128)(2,1)S(1)} fusion(bf16[1280,2048]{1,0:T(8,128)(2,1)S(1)} %bitcast.51, bf16[1280,2]{1,0:T(8,128)(2,1)S(1)} %collective-permute-done, bf16[1280,2050]{1,0:T(8,128)(2,1)S(1)} %constant_dynamic-update-slice_fusion, f32[2048]{0:T(1024)S(1)} %bitcast.55, f32[2048]{0:T(1024)S(1)} %bitcast.56, f32[2048]{0:T(1024)S(1)} %bitcast.53, ...), kind=kLoop, calls=%fused_computation.11 | loop fusion | flops 55050240 | bytes 21017600 | tf_op jit(solution)/shard_map/convert_element_type | solution.py:31
  30.2 0.0 copy-start.1
  30.2 2.3 copy-done.1
  32.6 0.4 fusion.32
  33.0 4.7 %collective-permute-start.2 = (bf16[384,2048]{1,0:T(8,128)(2,1)S(1)}, bf16[384,2048]{1,0:T(8,128)(2,1)}, u32[]{:S(2)}, u32[]{:S(2)}) collective-permute-start(bf16[384,2048]{1,0:T(8,128)(2,1)S(1)} %get-tuple-element.24), channel_id=1, source_target_pairs={{0,1},{1,2},{2,3},{3,4},{4,5},{5,6},{6,7},{7,8},{8,9},{9,10},{10,1... | collective-permute-start | bytes 4718600 | tf_op jit(solution)/shard_map/ppermute | solution.py:17
  37.7 1.3 collective-permute-start.3
  39.0 0.0 all-gather.2.cloned.1.call-update
  39.0 0.2 all-reduce.2.cloned.1.call-start
  39.2 0.1 compare_and_fusion.7
  39.4 33.0 %collective-permute-done.2 = bf16[384,2048]{1,0:T(8,128)(2,1)} collective-permute-done((bf16[384,2048]{1,0:T(8,128)(2,1)S(1)}, bf16[384,2048]{1,0:T(8,128)(2,1)}, u32[]{:S(2)}, u32[]{:S(2)}) %collective-permute-start.2) | collective-permute-done | bytes 1572896 | tf_op jit(solution)/shard_map/ppermute | solution.py:17
  72.4 5.8 %collective-permute-done.3 = bf16[384,2048]{1,0:T(8,128)(2,1)} collective-permute-done((bf16[384,2048]{1,0:T(8,128)(2,1)S(1)}, bf16[384,2048]{1,0:T(8,128)(2,1)}, u32[]{:S(2)}, u32[]{:S(2)}) %collective-permute-start.3) | collective-permute-done | bytes 1572896 | tf_op jit(solution)/shard_map/ppermute | solution.py:18
  78.1 7.5 %multiply_reduce_fusion = (f32[2048]{0:T(1024)S(1)}, bf16[2048,2048]{1,0:T(8,128)(2,1)}) fusion(bf16[384,2048]{1,0:T(8,128)(2,1)} %collective-permute-done.3, bf16[1280,2048]{1,0:T(8,128)(2,1)} %copy-done.1, bf16[384,2048]{1,0:T(8,128)(2,1)} %collective-permute-done.2), kind=kLoop, calls=%fused_computation.10 | loop fusion | flops 37746688 | bytes 16785408 | tf_op jit(solution)/shard_map/reduce_sum | solution.py:34
  85.6 8.2 %gather_fusion.2 = bf16[16,128,2048]{2,1,0:T(8,128)(2,1)} fusion(bf16[16,128,2048]{2,1,0:T(8,128)(2,1)} %bitcast.44, s32[1024]{0:T(1024)S(1)} %get-tuple-element.50), kind=kCustom, calls=%fused_computation.clone | custom fusion | bytes 16777280 | tf_op jit(solution)/shard_map/jit(_take)/gather | solution.py:47
  93.8 8.1 %gather_fusion.3 = bf16[16,128,2048]{2,1,0:T(8,128)(2,1)} fusion(bf16[16,128,2048]{2,1,0:T(8,128)(2,1)} %bitcast.45, s32[1024]{0:T(1024)S(1)} %get-tuple-element.49), kind=kCustom, calls=%fused_computation.2.clone | custom fusion | bytes 16777280 | tf_op jit(solution)/shard_map/jit(_take)/gather | solution.py:48
  102.0 8.3 %gather_fusion.4 = bf16[16,128,2048]{2,1,0:T(8,128)(2,1)} fusion(bf16[16,128,2048]{2,1,0:T(8,128)(2,1)} %bitcast.46, s32[1024]{0:T(1024)S(1)} %get-tuple-element.48), kind=kCustom, calls=%fused_computation.3.clone | custom fusion | bytes 16777280 | tf_op jit(solution)/shard_map/jit(_take)/gather | solution.py:47
  110.2 8.2 %gather_fusion.5 = bf16[16,128,2048]{2,1,0:T(8,128)(2,1)} fusion(bf16[16,128,2048]{2,1,0:T(8,128)(2,1)} %bitcast.47, s32[1024]{0:T(1024)S(1)} %get-tuple-element.47), kind=kCustom, calls=%fused_computation.4.clone | custom fusion | bytes 16777280 | tf_op jit(solution)/shard_map/jit(_take)/gather | solution.py:48
  118.4 8.2 %gather_fusion.6 = bf16[16,128,2048]{2,1,0:T(8,128)(2,1)} fusion(bf16[16,128,2048]{2,1,0:T(8,128)(2,1)} %bitcast.48, s32[1024]{0:T(1024)S(1)} %get-tuple-element.46), kind=kCustom, calls=%fused_computation.5.clone | custom fusion | bytes 16777280 | tf_op jit(solution)/shard_map/jit(_take)/gather | solution.py:47
  126.6 8.2 %gather_fusion.7 = bf16[16,128,2048]{2,1,0:T(8,128)(2,1)} fusion(bf16[16,128,2048]{2,1,0:T(8,128)(2,1)} %bitcast.49, s32[1024]{0:T(1024)S(1)} %get-tuple-element.45), kind=kCustom, calls=%fused_computation.6.clone | custom fusion | bytes 16777280 | tf_op jit(solution)/shard_map/jit(_take)/gather | solution.py:48
  134.8 8.4 %fusion.6 = f32[16,128,128]{2,1,0:T(8,128)S(1)} fusion(bf16[16,128,2048]{2,1,0:T(8,128)(2,1)} %gather_fusion.3, bf16[16,128,2048]{2,1,0:T(8,128)(2,1)} %gather_fusion.2, pred[16]{0:T(512)(128)(4,1)S(1)} %get-tuple-element.43, pred[16]{0:T(512)(128)(4,1)S(1)} %get-tuple-element.12), kind=kOutput, calls=%fused_computation.19 | convolution fusion | flops 1082130432 | bytes 17825824 | tf_op jit(solution)/shard_map/uwf,uvf->uwv/dot_general | solution.py:49
  143.2 8.4 %fusion.3 = f32[16,128,128]{2,1,0:T(8,128)S(1)} fusion(bf16[16,128,2048]{2,1,0:T(8,128)(2,1)} %gather_fusion.5, bf16[16,128,2048]{2,1,0:T(8,128)(2,1)} %gather_fusion.4, pred[16]{0:T(512)(128)(4,1)S(1)} %get-tuple-element.39, pred[16]{0:T(512)(128)(4,1)S(1)} %get-tuple-element.41), kind=kOutput, calls=%fused_computation.16 | convolution fusion | flops 1082130432 | bytes 17825824 | tf_op jit(solution)/shard_map/uwf,uvf->uwv/dot_general | solution.py:49
  151.6 8.4 %fusion = f32[16,128,128]{2,1,0:T(8,128)S(1)} fusion(bf16[16,128,2048]{2,1,0:T(8,128)(2,1)} %gather_fusion.7, bf16[16,128,2048]{2,1,0:T(8,128)(2,1)} %gather_fusion.6, pred[16]{0:T(512)(128)(4,1)S(1)} %get-tuple-element.35, pred[16]{0:T(512)(128)(4,1)S(1)} %get-tuple-element.37), kind=kOutput, calls=%fused_computation.13 | convolution fusion | flops 1082130432 | bytes 17825824 | tf_op jit(solution)/shard_map/uwf,uvf->uwv/dot_general | solution.py:49
  160.0 2.0 pad_maximum_fusion.2
  162.0 0.0 all-reduce.2.cloned.1.call-update
  162.7 0.8 gather_fusion
  163.6 27.1 %psum.15 = f32[2048]{0:T(1024)S(1)} all-reduce(f32[2048]{0:T(1024)S(1)} %get-tuple-element.10), channel_id=1, replica_groups=mesh['pix'=16,'ion'=16] {'pix'}, use_global_device_ids=true, to_apply=%region_2.0 | all-reduce | flops 2048 | bytes 16384 | tf_op jit(solution)/shard_map/psum | solution.py:36
  190.7 0.6 gather_fusion.9
  191.3 0.6 gather_fusion.8
  191.9 0.1 broadcast_select_fusion
  192.0 0.1 broadcast_select_fusion.1
  192.0 2.4 gather_fusion.1
  194.5 101.7 %all-reduce.2.cloned.1.call-done = f32[48,128,128]{2,1,0:T(8,128)} async-done(((f32[48,128,128]{2,1,0:T(8,128)}), f32[48,128,128]{2,1,0:T(8,128)}) %all-reduce.2.cloned.1.call-update) | async-done | bytes 3145744 | tf_op jit(solution)/shard_map/psum | solution.py:62
  296.2 3.0 fusion.19
  299.2 0.8 select_convert_fusion
  (18 shorter events, 0.1 us)
Async XLA Ops:
  8.0 154.7 %copy-start = (s32[160]{0:T(256)S(1)}, s32[160]{0:T(256)}, u32[]{:S(2)}) copy-start(s32[160]{0:T(256)} %param.14) | copy-start | bytes 1924
  8.0 13.4 %slice-start = ((s8[5242880]{0:T(1024)(128)(4,1)}), s8[1048576]{0:T(1024)(128)(4,1)S(1)}, s32[]{:S(2)}) async-start(s8[5242880]{0:T(1024)(128)(4,1)} %bitcast.50), calls=%async_computation.2 | async-start | bytes 2097152
  8.0 12.4 %copy-start.2 = (f32[5,2048]{1,0:T(8,128)S(1)}, f32[5,2048]{1,0:T(8,128)}, u32[]{:S(2)}) copy-start(f32[5,2048]{1,0:T(8,128)} %param.11) | copy-start | bytes 122884
  8.0 184.0 %all-gather.2.cloned.1.call-start = ((), (), s32[]{:S(2)}) async-start(), calls=%async_computation.1 | async-start | bytes 2228224 | tf_op jit(solution)/shard_map/all_gather | solution.py:38
  9.4 11.0 %collective-permute-start.1 = (bf16[1280,2]{1,0:T(8,128)(2,1)S(1)}, bf16[1280,2]{1,0:T(8,128)(2,1)S(1)}, u32[]{:S(2)}, u32[]{:S(2)}) collective-permute-start(bf16[1280,2]{1,0:T(8,128)(2,1)S(1)} %get-tuple-element.26), channel_id=1, source_target_pairs={{16,0},{32,16},{48,32},{64,48},{80,64},{96,80},{112,96},{128,112},... | collective-permute-start | bytes 15368 | tf_op jit(solution)/shard_map/ppermute | solution.py:18
  12.0 9.4 %slice-start.1 = ((s8[5242880]{0:T(1024)(128)(4,1)}), s8[4194304]{0:T(1024)(128)(4,1)S(1)}, s32[]{:S(2)}) async-start(s8[5242880]{0:T(1024)(128)(4,1)} %bitcast.50), calls=%async_computation.3 | async-start | bytes 8388608
  12.0 9.4 %collective-permute-start = (bf16[1280,2]{1,0:T(8,128)(2,1)S(1)}, bf16[1280,2]{1,0:T(8,128)(2,1)S(1)}, u32[]{:S(2)}, u32[]{:S(2)}) collective-permute-start(bf16[1280,2]{1,0:T(8,128)(2,1)S(1)} %get-tuple-element.27), channel_id=1, source_target_pairs={{0,16},{16,32},{32,48},{48,64},{64,80},{80,96},{96,112},{112,128},... | collective-permute-start | bytes 15368 | tf_op jit(solution)/shard_map/ppermute | solution.py:17
  21.4 17.9 %copy-start.3 = (s32[48,2]{0,1:T(2,128)S(1)}, s32[48,2]{0,1:T(2,128)}, u32[]{:S(2)}) copy-start(s32[48,2]{0,1:T(2,128)} %param.12) | copy-start | bytes 1156
  30.2 2.4 copy-start.1
  33.0 39.4 %collective-permute-start.2 = (bf16[384,2048]{1,0:T(8,128)(2,1)S(1)}, bf16[384,2048]{1,0:T(8,128)(2,1)}, u32[]{:S(2)}, u32[]{:S(2)}) collective-permute-start(bf16[384,2048]{1,0:T(8,128)(2,1)S(1)} %get-tuple-element.24), channel_id=1, source_target_pairs={{0,1},{1,2},{2,3},{3,4},{4,5},{5,6},{6,7},{7,8},{8,9},{9,10},{10,1... | collective-permute-start | bytes 4718600 | tf_op jit(solution)/shard_map/ppermute | solution.py:17
  37.7 40.5 %collective-permute-start.3 = (bf16[384,2048]{1,0:T(8,128)(2,1)S(1)}, bf16[384,2048]{1,0:T(8,128)(2,1)}, u32[]{:S(2)}, u32[]{:S(2)}) collective-permute-start(bf16[384,2048]{1,0:T(8,128)(2,1)S(1)} %get-tuple-element.25), channel_id=1, source_target_pairs={{1,0},{2,1},{3,2},{4,3},{5,4},{6,5},{7,6},{8,7},{9,8},{10,9},{11,1... | collective-permute-start | bytes 4718600 | tf_op jit(solution)/shard_map/ppermute | solution.py:18
  39.0 257.2 %all-reduce.2.cloned.1.call-start = ((), (), s32[]{:S(2)}) async-start(), calls=%async_computation | async-start | bytes 6291456 | tf_op jit(solution)/shard_map/psum | solution.py:62
Sparse Core Ops, SparseCore 0:
  39.1 102.5 all-gather.1
Sparse Core Ops, SparseCore 1:
  162.1 134.0 all-reduce.1
where the time goes:
time: 308 us; the launch traced here: 307 us
  waiting for transfers between devices  141 us (46%)
  local copies, waits for them, and re-layouts  60.8 us (20%)
  matrix products  28.1 us (9%)
  blocking collectives  27.1 us (9%)
  other arithmetic  19.4 us (6%)
  between operations  16.4 us (5%)
  starting transfers between devices  14.2 us (5%)
    psum x1, waiting for transfers between devices, on_device(): gram = lax.psum(grams, 'pix')  102 us
    ppermute x2, waiting for transfers between devices, extended_2(): before = lax.ppermute(last, axis, up)  33.8 us
    psum x1, blocking collectives, on_device(): energy = lax.psum(squares, 'pix') / pixel_count  27.1 us
    dot_general x3, matrix products, group_gram(): jnp.einsum('uwf,uvf->uwv', left_operand, right_operand, preferred_element...  25.1 us
    gather x3, local copies, waits for them, and re-layouts, group_gram(): left_operand = jnp.take(ext_blocks, chosen[:, 0], axis=0)  24.7 us
    gather x3, local copies, waits for them, and re-layouts, group_gram(): right_operand = jnp.take(ext_blocks, chosen[:, 1], axis=0)  24.5 us
    ppermute x2, starting transfers between devices, extended_2(): before = lax.ppermute(last, axis, up)  10.1 us
    convert_element_type x1, other arithmetic, on_device(): smoothed = total.astype(jnp.bfloat16)  8.82 us
  transfers between devices with their start and end apart: 6, of which 4 were waited for; matrix products, arithmetic and copies ran while one was open for 30% of the time, Pallas kernels for 0%

commit v1 on v0

--- a/solution.py
+++ b/solution.py
@@ -59,7 +59,8 @@
     matrices = jnp.take(lookup_tables, rules, axis=0)
     share = block // lax.axis_size("pix")
     offset = lax.axis_index("pix") * share
-    gram = lax.psum(grams, "pix")
+    parts = lax.all_gather(grams, "pix", axis=0, tiled=False)
+    gram = parts.sum(axis=0)
     coloc = (gram * inv_left[:, :, None] * inv_right[:, None, :] / pixel_count).astype(jnp.bfloat16)
     complete_scores = jnp.einsum(
         "src,scd->srd", coloc, matrices, preferred_element_type=jnp.float32

time: 308 us -> 446 us (1.45)
  waiting for transfers between devices: 141 us -> 261 us
  other arithmetic: 19.4 us -> 36.6 us
    all_gather x0 -> x1, waiting for transfers between devices: none -> 221 us  [on_device(): parts = lax.all_gather(grams, 'pix', axis=0, tiled=False)]
    psum x1 -> x0, waiting for transfers between devices: 102 us -> none  [on_device(): gram = lax.psum(grams, 'pix')]
    reduce_sum x0 -> x1, other arithmetic: none -> 17.3 us  [on_device(): gram = parts.sum(axis=0)]
  transfers between devices with their start and end apart: 6 -> 6, of which waited for: 4 -> 4; matrix products, arithmetic and copies ran while one was open for 30% -> 21% of each run, Pallas kernels for 0% -> 0%
where the time goes in v1:
time: 446 us; the launch traced here: 444 us
  waiting for transfers between devices  261 us (59%)
  local copies, waits for them, and re-layouts  62 us (14%)
  other arithmetic  36.6 us (8%)
  matrix products  27.6 us (6%)
  blocking collectives  27.5 us (6%)
  between operations  15 us (3%)
  starting transfers between devices  14.2 us (3%)
    all_gather x1, waiting for transfers between devices, on_device(): parts = lax.all_gather(grams, 'pix', axis=0, tiled=False)  221 us
    ppermute x2, waiting for transfers between devices, extended_2(): before = lax.ppermute(last, axis, up)  33.8 us
    psum x1, blocking collectives, on_device(): energy = lax.psum(squares, 'pix') / pixel_count  27.5 us
    dot_general x3, matrix products, group_gram(): jnp.einsum('uwf,uvf->uwv', left_operand, right_operand, preferred_element...  25.2 us
    gather x3, local copies, waits for them, and re-layouts, group_gram(): left_operand = jnp.take(ext_blocks, chosen[:, 0], axis=0)  24.7 us
    gather x3, local copies, waits for them, and re-layouts, group_gram(): right_operand = jnp.take(ext_blocks, chosen[:, 1], axis=0)  24.5 us
    reduce_sum x1, other arithmetic, on_device(): gram = parts.sum(axis=0)  17.3 us
    ppermute x2, starting transfers between devices, extended_2(): before = lax.ppermute(last, axis, up)  10.1 us
  transfers between devices with their start and end apart: 6, of which 4 were waited for; matrix products, arithmetic and copies ran while one was open for 21% of the time, Pallas kernels for 0%

profile of v1, /device:TPU:7, one launch (start us, length us, event | category | flops | bytes accessed | tf_op | source)
XLA Modules:
  0.0 443.6 jit_solution(4695164438002046226)
XLA Ops:
  7.2 0.0 copy-start
  7.2 0.0 slice-start
  7.2 0.0 copy-start.2
  7.2 0.0 all-gather.4.cloned.1.call-start
  7.2 1.3 fusion.33
  8.6 2.6 collective-permute-start.1
  11.2 0.0 slice-start.1
  11.2 5.4 %collective-permute-start = (bf16[1280,2]{1,0:T(8,128)(2,1)S(1)}, bf16[1280,2]{1,0:T(8,128)(2,1)S(1)}, u32[]{:S(2)}, u32[]{:S(2)}) collective-permute-start(bf16[1280,2]{1,0:T(8,128)(2,1)S(1)} %get-tuple-element.27), channel_id=1, source_target_pairs={{0,16},{16,32},{32,48},{48,64},{64,80},{80,96},{96,112},{112,128},... | collective-permute-start | bytes 15368 | tf_op jit(solution)/shard_map/ppermute | solution.py:17
  16.5 3.0 constant_dynamic-update-slice_fusion.1
  19.6 0.0 copy-done.2
  19.6 0.0 collective-permute-done.1
  19.6 0.1 constant_dynamic-update-slice_fusion
  19.7 0.8 collective-permute-done
  20.5 8.8 %add_convert_fusion = bf16[1280,2048]{1,0:T(8,128)(2,1)S(1)} fusion(bf16[1280,2048]{1,0:T(8,128)(2,1)S(1)} %bitcast.53, bf16[1280,2]{1,0:T(8,128)(2,1)S(1)} %collective-permute-done, bf16[1280,2050]{1,0:T(8,128)(2,1)S(1)} %constant_dynamic-update-slice_fusion, f32[2048]{0:T(1024)S(1)} %bitcast.57, f32[2048]{0:T(1024)S(1)} %bitcast.58, f32[2048]{0:T(1024)S(1)} %bitcast.55, ...), kind=kLoop, calls=%fused_computation.11 | loop fusion | flops 55050240 | bytes 21017600 | tf_op jit(solution)/shard_map/convert_element_type | solution.py:31
  29.4 0.0 copy-start.1
  29.4 2.3 copy-done.1
  31.7 0.4 fusion.32
  32.1 4.7 %collective-permute-start.2 = (bf16[384,2048]{1,0:T(8,128)(2,1)S(1)}, bf16[384,2048]{1,0:T(8,128)(2,1)}, u32[]{:S(2)}, u32[]{:S(2)}) collective-permute-start(bf16[384,2048]{1,0:T(8,128)(2,1)S(1)} %get-tuple-element.24), channel_id=1, source_target_pairs={{0,1},{1,2},{2,3},{3,4},{4,5},{5,6},{6,7},{7,8},{8,9},{9,10},{10,1... | collective-permute-start | bytes 4718600 | tf_op jit(solution)/shard_map/ppermute | solution.py:17
  36.8 1.3 collective-permute-start.3
  38.1 0.0 all-gather.4.cloned.1.call-update
  38.2 0.2 all-gather.6.cloned.1.call-start
  38.4 0.1 compare_and_fusion.7
  38.5 33.0 %collective-permute-done.2 = bf16[384,2048]{1,0:T(8,128)(2,1)} collective-permute-done((bf16[384,2048]{1,0:T(8,128)(2,1)S(1)}, bf16[384,2048]{1,0:T(8,128)(2,1)}, u32[]{:S(2)}, u32[]{:S(2)}) %collective-permute-start.2) | collective-permute-done | bytes 1572896 | tf_op jit(solution)/shard_map/ppermute | solution.py:17
  71.5 5.8 %collective-permute-done.3 = bf16[384,2048]{1,0:T(8,128)(2,1)} collective-permute-done((bf16[384,2048]{1,0:T(8,128)(2,1)S(1)}, bf16[384,2048]{1,0:T(8,128)(2,1)}, u32[]{:S(2)}, u32[]{:S(2)}) %collective-permute-start.3) | collective-permute-done | bytes 1572896 | tf_op jit(solution)/shard_map/ppermute | solution.py:18
  77.3 7.5 %multiply_reduce_fusion = (f32[2048]{0:T(1024)S(1)}, bf16[2048,2048]{1,0:T(8,128)(2,1)}) fusion(bf16[384,2048]{1,0:T(8,128)(2,1)} %collective-permute-done.3, bf16[1280,2048]{1,0:T(8,128)(2,1)} %copy-done.1, bf16[384,2048]{1,0:T(8,128)(2,1)} %collective-permute-done.2), kind=kLoop, calls=%fused_computation.10 | loop fusion | flops 37746688 | bytes 16785408 | tf_op jit(solution)/shard_map/reduce_sum | solution.py:34
  84.8 8.2 %gather_fusion.2 = bf16[16,128,2048]{2,1,0:T(8,128)(2,1)} fusion(bf16[16,128,2048]{2,1,0:T(8,128)(2,1)} %bitcast.45, s32[1024]{0:T(1024)S(1)} %get-tuple-element.50), kind=kCustom, calls=%fused_computation.clone | custom fusion | bytes 16777280 | tf_op jit(solution)/shard_map/jit(_take)/gather | solution.py:47
  93.0 8.1 %gather_fusion.3 = bf16[16,128,2048]{2,1,0:T(8,128)(2,1)} fusion(bf16[16,128,2048]{2,1,0:T(8,128)(2,1)} %bitcast.46, s32[1024]{0:T(1024)S(1)} %get-tuple-element.49), kind=kCustom, calls=%fused_computation.2.clone | custom fusion | bytes 16777280 | tf_op jit(solution)/shard_map/jit(_take)/gather | solution.py:48
  101.1 8.3 %gather_fusion.4 = bf16[16,128,2048]{2,1,0:T(8,128)(2,1)} fusion(bf16[16,128,2048]{2,1,0:T(8,128)(2,1)} %bitcast.47, s32[1024]{0:T(1024)S(1)} %get-tuple-element.48), kind=kCustom, calls=%fused_computation.3.clone | custom fusion | bytes 16777280 | tf_op jit(solution)/shard_map/jit(_take)/gather | solution.py:47
  109.4 8.2 %gather_fusion.5 = bf16[16,128,2048]{2,1,0:T(8,128)(2,1)} fusion(bf16[16,128,2048]{2,1,0:T(8,128)(2,1)} %bitcast.48, s32[1024]{0:T(1024)S(1)} %get-tuple-element.47), kind=kCustom, calls=%fused_computation.4.clone | custom fusion | bytes 16777280 | tf_op jit(solution)/shard_map/jit(_take)/gather | solution.py:48
  117.6 8.2 %gather_fusion.6 = bf16[16,128,2048]{2,1,0:T(8,128)(2,1)} fusion(bf16[16,128,2048]{2,1,0:T(8,128)(2,1)} %bitcast.49, s32[1024]{0:T(1024)S(1)} %get-tuple-element.46), kind=kCustom, calls=%fused_computation.5.clone | custom fusion | bytes 16777280 | tf_op jit(solution)/shard_map/jit(_take)/gather | solution.py:47
  125.8 8.2 %gather_fusion.7 = bf16[16,128,2048]{2,1,0:T(8,128)(2,1)} fusion(bf16[16,128,2048]{2,1,0:T(8,128)(2,1)} %bitcast.50, s32[1024]{0:T(1024)S(1)} %get-tuple-element.45), kind=kCustom, calls=%fused_computation.6.clone | custom fusion | bytes 16777280 | tf_op jit(solution)/shard_map/jit(_take)/gather | solution.py:48
  134.0 8.4 %fusion.6 = f32[16,128,128]{2,1,0:T(8,128)S(1)} fusion(bf16[16,128,2048]{2,1,0:T(8,128)(2,1)} %gather_fusion.3, bf16[16,128,2048]{2,1,0:T(8,128)(2,1)} %gather_fusion.2, pred[16]{0:T(512)(128)(4,1)S(1)} %get-tuple-element.43, pred[16]{0:T(512)(128)(4,1)S(1)} %get-tuple-element.12), kind=kOutput, calls=%fused_computation.19 | convolution fusion | flops 1082130432 | bytes 17825824 | tf_op jit(solution)/shard_map/uwf,uvf->uwv/dot_general | solution.py:49
  142.4 8.4 %fusion.3 = f32[16,128,128]{2,1,0:T(8,128)S(1)} fusion(bf16[16,128,2048]{2,1,0:T(8,128)(2,1)} %gather_fusion.5, bf16[16,128,2048]{2,1,0:T(8,128)(2,1)} %gather_fusion.4, pred[16]{0:T(512)(128)(4,1)S(1)} %get-tuple-element.39, pred[16]{0:T(512)(128)(4,1)S(1)} %get-tuple-element.41), kind=kOutput, calls=%fused_computation.16 | convolution fusion | flops 1082130432 | bytes 17825824 | tf_op jit(solution)/shard_map/uwf,uvf->uwv/dot_general | solution.py:49
  150.8 8.4 %fusion = f32[16,128,128]{2,1,0:T(8,128)S(1)} fusion(bf16[16,128,2048]{2,1,0:T(8,128)(2,1)} %gather_fusion.7, bf16[16,128,2048]{2,1,0:T(8,128)(2,1)} %gather_fusion.6, pred[16]{0:T(512)(128)(4,1)S(1)} %get-tuple-element.35, pred[16]{0:T(512)(128)(4,1)S(1)} %get-tuple-element.37), kind=kOutput, calls=%fused_computation.13 | convolution fusion | flops 1082130432 | bytes 17825824 | tf_op jit(solution)/shard_map/uwf,uvf->uwv/dot_general | solution.py:49
  159.2 2.0 pad_maximum_fusion.2
  161.1 0.0 all-gather.6.cloned.1.call-update
  161.8 0.0 copy-done
  161.9 0.8 gather_fusion
  162.7 27.5 %psum.7 = f32[2048]{0:T(1024)S(1)} all-reduce(f32[2048]{0:T(1024)S(1)} %get-tuple-element.10), channel_id=1, replica_groups=mesh['pix'=16,'ion'=16] {'pix'}, use_global_device_ids=true, to_apply=%region_2.0 | all-reduce | flops 2048 | bytes 16384 | tf_op jit(solution)/shard_map/psum | solution.py:36
  190.3 0.6 gather_fusion.9
  190.8 0.6 gather_fusion.8
  191.4 0.1 broadcast_select_fusion
  191.5 0.1 broadcast_select_fusion.1
  191.6 3.6 gather_fusion.1
  195.2 221.1 %all-gather.6.cloned.1.call-done = f32[768,128,128]{2,1,0:T(8,128)} async-done(((f32[48,128,128]{2,1,0:T(8,128)}), f32[768,128,128]{2,1,0:T(8,128)}) %all-gather.6.cloned.1.call-update) | async-done | bytes 50331664 | tf_op jit(solution)/shard_map/all_gather | solution.py:62
  416.3 17.3 %reduce_sum.18 = f32[48,128,128]{2,1,0:T(8,128)S(1)} reduce(f32[16,48,128,128]{3,2,1,0:T(8,128)} %bitcast.51, f32[]{:T(128)} %constant.40.clone.1), dimensions={0}, to_apply=%region_0.2 | reduce | flops 11796480 | bytes 53477380 | tf_op jit(solution)/shard_map/reduce_sum | solution.py:63
  433.5 2.5 fusion.19
  436.0 0.8 select_convert_fusion
  (19 shorter events, 0.1 us)
Async XLA Ops:
  7.2 154.7 %copy-start = (s32[160]{0:T(256)S(1)}, s32[160]{0:T(256)}, u32[]{:S(2)}) copy-start(s32[160]{0:T(256)} %param.14) | copy-start | bytes 1924
  7.2 13.4 %slice-start = ((s8[5242880]{0:T(1024)(128)(4,1)}), s8[1048576]{0:T(1024)(128)(4,1)S(1)}, s32[]{:S(2)}) async-start(s8[5242880]{0:T(1024)(128)(4,1)} %bitcast.52), calls=%async_computation.2 | async-start | bytes 2097152
  7.2 12.4 %copy-start.2 = (f32[5,2048]{1,0:T(8,128)S(1)}, f32[5,2048]{1,0:T(8,128)}, u32[]{:S(2)}) copy-start(f32[5,2048]{1,0:T(8,128)} %param.11) | copy-start | bytes 122884
  7.2 184.4 %all-gather.4.cloned.1.call-start = ((), (), s32[]{:S(2)}) async-start(), calls=%async_computation | async-start | bytes 2228224 | tf_op jit(solution)/shard_map/all_gather | solution.py:38
  8.6 11.0 %collective-permute-start.1 = (bf16[1280,2]{1,0:T(8,128)(2,1)S(1)}, bf16[1280,2]{1,0:T(8,128)(2,1)S(1)}, u32[]{:S(2)}, u32[]{:S(2)}) collective-permute-start(bf16[1280,2]{1,0:T(8,128)(2,1)S(1)} %get-tuple-element.26), channel_id=1, source_target_pairs={{16,0},{32,16},{48,32},{64,48},{80,64},{96,80},{112,96},{128,112},... | collective-permute-start | bytes 15368 | tf_op jit(solution)/shard_map/ppermute | solution.py:18
  11.2 9.4 %slice-start.1 = ((s8[5242880]{0:T(1024)(128)(4,1)}), s8[4194304]{0:T(1024)(128)(4,1)S(1)}, s32[]{:S(2)}) async-start(s8[5242880]{0:T(1024)(128)(4,1)} %bitcast.52), calls=%async_computation.3 | async-start | bytes 8388608
  11.2 9.4 %collective-permute-start = (bf16[1280,2]{1,0:T(8,128)(2,1)S(1)}, bf16[1280,2]{1,0:T(8,128)(2,1)S(1)}, u32[]{:S(2)}, u32[]{:S(2)}) collective-permute-start(bf16[1280,2]{1,0:T(8,128)(2,1)S(1)} %get-tuple-element.27), channel_id=1, source_target_pairs={{0,16},{16,32},{32,48},{48,64},{64,80},{80,96},{96,112},{112,128},... | collective-permute-start | bytes 15368 | tf_op jit(solution)/shard_map/ppermute | solution.py:17
  20.5 17.9 %copy-start.3 = (s32[48,2]{0,1:T(2,128)S(1)}, s32[48,2]{0,1:T(2,128)}, u32[]{:S(2)}) copy-start(s32[48,2]{0,1:T(2,128)} %param.12) | copy-start | bytes 1156
  29.4 2.4 copy-start.1
  32.1 39.4 %collective-permute-start.2 = (bf16[384,2048]{1,0:T(8,128)(2,1)S(1)}, bf16[384,2048]{1,0:T(8,128)(2,1)}, u32[]{:S(2)}, u32[]{:S(2)}) collective-permute-start(bf16[384,2048]{1,0:T(8,128)(2,1)S(1)} %get-tuple-element.24), channel_id=1, source_target_pairs={{0,1},{1,2},{2,3},{3,4},{4,5},{5,6},{6,7},{7,8},{8,9},{9,10},{10,1... | collective-permute-start | bytes 4718600 | tf_op jit(solution)/shard_map/ppermute | solution.py:17
  36.8 40.5 %collective-permute-start.3 = (bf16[384,2048]{1,0:T(8,128)(2,1)S(1)}, bf16[384,2048]{1,0:T(8,128)(2,1)}, u32[]{:S(2)}, u32[]{:S(2)}) collective-permute-start(bf16[384,2048]{1,0:T(8,128)(2,1)S(1)} %get-tuple-element.25), channel_id=1, source_target_pairs={{1,0},{2,1},{3,2},{4,3},{5,4},{6,5},{7,6},{8,7},{9,8},{10,9},{11,1... | collective-permute-start | bytes 4718600 | tf_op jit(solution)/shard_map/ppermute | solution.py:18
  38.2 378.1 %all-gather.6.cloned.1.call-start = ((), (), s32[]{:S(2)}) async-start(), calls=%async_computation.1 | async-start | bytes 53477376 | tf_op jit(solution)/shard_map/all_gather | solution.py:62
Sparse Core Ops, SparseCore 0:
  38.3 102.5 all-gather.3
  161.3 254.9 all-gather.5
